TPU v7x, 256 devices: a whole 4x4x8 slice. The times are simulated.
256 devices in a mesh: layer: 32 (over y, z), row: 2 (over core), col: 4 (over x).
Axes of the slice: x: 4, y: 4, z: 8, core: 2. Of those that a mesh axis runs over, the one named last changes fastest.
Arguments:
- lpanel: bfloat16 [32, 8, 3072, 256], P('layer', None, 'row', 'col'), may hold values from -6 to 6
- upanel: bfloat16 [32, 8, 256, 3072], P('layer', None, 'row', 'col'), may hold values from -0.03125 to 0.03125
- lpat: int32 [32, 8, 24], P('layer', None, 'row'), may hold values 0 or 1
- upat: int32 [32, 8, 24], P('layer', None, 'col'), may hold values 0 or 1
- ancestor_entries: float32 [3072, 3072], P('row', 'col'), may hold values from -2 to 64, as said below
Outputs:
- schur: float32 [3072, 3072], P(('row', 'layer'), 'col')
- diag_lu: float32 [24, 128, 128], P('col')
Inputs may be any that keep to these rules, and one draw needn't show every extreme that they name: `ancestor_entries`: entries on the diagonal lie in 32 to 64; all other entries in -2 to 2.
All inputs are finite; a program needn't handle non-finite values. No bound on the sum of `lpat` or of `upat` on one device may be relied on, other than what follows from the above.
Results may differ from a plain program's by a relative error of at most 0.0003.
Values may be sent and summed in bfloat16 or wider, within the bound.
A program may use at most 64 MiB of HBM per device.

v0:
```python
import jax
import jax.numpy as jnp
from jax import lax
from jax.sharding import PartitionSpec as P

BLK = 128


panel_width = 16


def mask_rows(panel, pattern, block):
    count, length, inner = panel.shape
    shaped = panel.reshape(count, length // block, block, inner)
    return (shaped * pattern[:, :, None, None].astype(panel.dtype)).reshape(count, length, inner)


def mask_cols(panel, pattern, block):
    count, inner, length = panel.shape
    shaped = panel.reshape(count, inner, length // block, block)
    return (shaped * pattern[:, None, :, None].astype(panel.dtype)).reshape(count, inner, length)


def eliminate_tall(tile, steps):
    row_places = jnp.arange(tile.shape[1])
    col_places = jnp.arange(tile.shape[2])

    def eliminate_sweep(step, current):
        pivot = current[:, step, step]
        below = row_places > step
        column = jnp.where(below[None, :], current[:, :, step] / pivot[:, None], 0.0)
        right = col_places > step
        row_part = jnp.where(right[None, :], current[:, step, :], 0.0)
        current = current - column[:, :, None] * row_part[:, None, :]
        placed = below[None, :, None] & (col_places == step)[None, None, :]
        return jnp.where(placed, column[:, :, None], current)

    return lax.fori_loop(0, steps, eliminate_sweep, tile)


def forward_rows(unit, strip):
    places = jnp.arange(unit.shape[1])

    def forward_sweep(step, current):
        factors = jnp.where(places[None, :] > step, unit[:, :, step], 0.0)
        return current - factors[:, :, None] * current[:, step, :][:, None, :]

    return lax.fori_loop(0, unit.shape[1], forward_sweep, strip)


def factor(blocks):
    size = blocks.shape[-1]
    current = blocks
    for offset in range(0, size, panel_width):
        end = offset + panel_width
        panel = eliminate_tall(current[:, offset:, offset:end], panel_width)
        current = current.at[:, offset:, offset:end].set(panel)
        if end < size:
            strip = forward_rows(panel[:, :panel_width, :], current[:, offset:end, end:])
            current = current.at[:, offset:end, end:].set(strip)
            lower = panel[:, panel_width:, :]
            trailing = current[:, end:, end:] - jnp.einsum(
                "bik,bkj->bij",
                lower,
                strip,
                precision=lax.Precision.HIGHEST,
                preferred_element_type=jnp.float32,
            )
            current = current.at[:, end:, end:].set(trailing)
    return current


def candidates(matrix):
    width = matrix.shape[1]
    per_group = lax.axis_size("col") // lax.axis_size("row")
    column = lax.axis_index("col")
    valid = column // per_group == lax.axis_index("row")
    begin = column % per_group * width
    square = lax.dynamic_slice_in_dim(matrix, begin, width, 0)
    count = width // BLK
    blocks = jnp.stack(
        [square[j * BLK : (j + 1) * BLK, j * BLK : (j + 1) * BLK] for j in range(count)]
    )
    return (blocks, valid)


def pick_owned(gathered):
    per_group = lax.axis_size("col") // lax.axis_size("row")
    count = gathered.shape[0] // lax.axis_size("row")
    source = lax.axis_index("col") // per_group
    return lax.dynamic_slice_in_dim(gathered, source * count, count, 0)


def shards(lpanel, upanel, lpat, upat, ancestor_entries):
    left_masked = mask_rows(lpanel[0], lpat[0], BLK)
    right_masked = mask_cols(upanel[0], upat[0], BLK)
    right_full = lax.all_gather(right_masked, "row", axis=1, tiled=True)
    length = left_masked.shape[1]
    update = jnp.einsum(
        "kmw,kwn->mn",
        lax.all_gather(left_masked, "col", axis=2, tiled=True),
        right_full,
        preferred_element_type=jnp.float32,
    )
    share_rows = length // lax.axis_size("layer")
    offset = lax.axis_index("layer") * share_rows
    total = lax.psum(update, "layer")
    summed = ancestor_entries - total
    schur = lax.dynamic_slice_in_dim(summed, offset, share_rows, 0)
    pivots, valid = candidates(summed)
    diag_lu = factor(pick_owned(lax.all_gather(pivots, "row", axis=0, tiled=True)))
    return (schur, diag_lu)


def solution(mesh):
    return jax.shard_map(
        shards,
        mesh=mesh,
        in_specs=(
            P("layer", None, "row", "col"),
            P("layer", None, "row", "col"),
            P("layer", None, "row"),
            P("layer", None, "col"),
            P("row", "col"),
        ),
        out_specs=(P(("row", "layer"), "col"), P("col", None, None)),
        check_vma=False,
    )
```

profile of v0, /device:TPU:2, one launch (start us, length us, event | category | flops | bytes accessed | tf_op | source)
XLA Modules:
  0.0 483.3 jit_solution(14656002472003928525)
XLA Ops:
  7.2 0.9 copy.122
  8.3 2.7 bitcast_multiply_fusion
  11.2 1.4 bitcast_multiply_fusion.1
  12.6 18.9 %all-gather.5.cloned.1.call-done = bf16[8,256,768]{2,1,0:T(8,128)(2,1)} async-done(((bf16[8,128,768]{2,1,0:T(8,128)(2,1)}), bf16[8,256,768]{2,1,0:T(8,128)(2,1)}) %all-gather.5.cloned.1.call-update) | async-done | bytes 3145744 | tf_op jit(solution)/shard_map/all_gather | solution.py:97
  31.5 71.0 %all-gather.3.cloned.1.call-done = bf16[8,1536,256]{1,2,0:T(8,128)(2,1)} async-done(((bf16[8,1536,64]{1,2,0:T(8,128)(2,1)}), bf16[8,1536,256]{1,2,0:T(8,128)(2,1)}) %all-gather.3.cloned.1.call-update) | async-done | bytes 6291472 | tf_op jit(solution)/shard_map/all_gather | solution.py:101
  102.5 9.7 %convolution_bitcast_fusion = f32[1536,768]{1,0:T(8,128)} fusion(bf16[8,1536,256]{1,2,0:T(8,128)(2,1)} %all-gather.3.cloned.1.call-done, bf16[8,256,768]{2,1,0:T(8,128)(2,1)} %all-gather.5.cloned.1.call-done), kind=kOutput, calls=%fused_computation.119 | convolution fusion | flops 4831838208 | bytes 14155776 | tf_op jit(solution)/shard_map/kmw,kwn->mn/dot_general | solution.py:99
  113.6 167.2 %all-reduce.2.cloned.1.call-done = f32[1536,768]{1,0:T(8,128)} async-done(((f32[1536,768]{1,0:T(8,128)}), f32[1536,768]{1,0:T(8,128)}) %all-reduce.2.cloned.1.call-update) | async-done | bytes 4718608 | tf_op jit(solution)/shard_map/psum | solution.py:107
  280.8 4.4 sub.134
  285.4 2.5 all_gather.11
  288.2 13.2 %while.248 = (s32[]{:T(128)}, f32[6,128,16]{1,0,2:T(8,128)S(1)}, s32[]{:T(128)}) while((s32[]{:T(128)}, f32[6,128,16]{1,0,2:T(8,128)S(1)}, s32[]{:T(128)}) %tuple.580), condition=%wide.region_2.3_spmd.clone.clone, body=%wide.region_1.2_spmd.clone.clone.sunk | while | flops 40706 | bytes 212433 | solution.py:38
  301.5 2.6 while.241
  304.2 2.1 dynamic-slice_select_fusion
  306.3 6.4 %scatter.75 = f32[6,128,128]{1,2,0:T(8,128)S(1)} dynamic-update-slice(f32[6,128,128]{1,2,0:T(8,128)S(1)} %get-tuple-element.1863, f32[6,16,112]{1,2,0:T(8,128)S(1)} %dynamic-slice_select_fusion, s32[]{:T(128)} %constant.1116.clone.1, s32[]{:T(128)} %bitcast.13, s32[]{:T(128)} %bitcast.14) | dynamic-update-slice | bytes 86020 | tf_op jit(solution)/shard_map/scatter | solution.py:60
  313.5 7.3 %scatter.76 = f32[6,128,128]{1,2,0:T(8,128)S(1)} dynamic-update-slice(f32[6,128,128]{1,2,0:T(8,128)S(1)} %scatter.75, f32[6,112,112]{1,2,0:T(8,128)S(1)} %convolution_subtract_fusion, s32[]{:T(128)} %constant.1116.clone.1, s32[]{:T(128)} %constant.1125.clone.1, s32[]{:T(128)} %constant.1125.clone.1) | dynamic-update-slice | bytes 602116 | tf_op jit(solution)/shard_map/scatter | solution.py:69
  320.8 12.9 %while.249 = (s32[]{:T(128)}, f32[6,112,16]{1,0,2:T(8,128)S(1)}, s32[]{:T(128)}) while((s32[]{:T(128)}, f32[6,112,16]{1,0,2:T(8,128)S(1)}, s32[]{:T(128)}) %tuple.586), condition=%wide.region_7.8_spmd.clone.clone, body=%wide.region_6.7_spmd.clone.clone.sunk | while | flops 35634 | bytes 186145 | solution.py:38
  333.7 2.3 scatter.79
  336.3 2.5 while.242
  339.0 3.2 scatter.80
  342.9 3.2 scatter.81
  346.2 12.5 %while.250 = (s32[]{:T(128)}, f32[6,96,16]{1,0,2:T(8,128)S(1)}, s32[]{:T(128)}) while((s32[]{:T(128)}, f32[6,96,16]{1,0,2:T(8,128)S(1)}, s32[]{:T(128)}) %tuple.592), condition=%wide.region_11.12_spmd.clone.clone, body=%wide.region_10.11_spmd.clone.clone.sunk | while | flops 30562 | bytes 159857 | solution.py:38
  358.7 2.3 scatter.84
  361.2 2.6 while.243
  363.9 3.0 scatter.85
  367.6 3.0 scatter.86
  370.6 12.1 %while.251 = (s32[]{:T(128)}, f32[6,80,16]{1,0,2:T(8,128)S(1)}, s32[]{:T(128)}) while((s32[]{:T(128)}, f32[6,80,16]{1,0,2:T(8,128)S(1)}, s32[]{:T(128)}) %tuple.598), condition=%wide.region_15.16_spmd.clone.clone, body=%wide.region_14.15_spmd.clone.clone.sunk | while | flops 25490 | bytes 133569 | solution.py:38
  382.8 2.3 scatter.89
  385.3 2.5 while.244
  388.0 3.0 scatter.90
  391.5 2.8 scatter.91
  394.4 11.8 %while.252 = (s32[]{:T(128)}, f32[6,64,16]{1,0,2:T(8,128)S(1)}, s32[]{:T(128)}) while((s32[]{:T(128)}, f32[6,64,16]{1,0,2:T(8,128)S(1)}, s32[]{:T(128)}) %tuple.604), condition=%wide.region_19.20_spmd.clone.clone, body=%wide.region_18.19_spmd.clone.clone.sunk | while | flops 20418 | bytes 107281 | solution.py:38
  406.2 2.3 scatter.94
  408.7 2.5 while.245
  411.4 2.6 scatter.95
  414.5 2.6 scatter.96
  417.2 11.5 %while.253 = (s32[]{:T(128)}, f32[6,48,16]{1,0,2:T(8,128)S(1)}, s32[]{:T(128)}) while((s32[]{:T(128)}, f32[6,48,16]{1,0,2:T(8,128)S(1)}, s32[]{:T(128)}) %tuple.610), condition=%wide.region_23.24_spmd.clone.clone, body=%wide.region_22.23_spmd.clone.clone.sunk | while | flops 15346 | bytes 80993 | solution.py:38
  428.6 2.3 scatter.99
  431.1 2.5 while.246
  433.8 2.4 scatter.100
  436.6 2.4 scatter.101
  439.1 11.1 %while.254 = (s32[]{:T(128)}, f32[6,32,16]{1,0,2:T(8,128)S(1)}, s32[]{:T(128)}) while((s32[]{:T(128)}, f32[6,32,16]{1,0,2:T(8,128)S(1)}, s32[]{:T(128)}) %tuple.616), condition=%wide.region_27.28_spmd.clone.clone, body=%wide.region_26.27_spmd.clone.clone.sunk | while | flops 10274 | bytes 54705 | solution.py:38
  450.4 2.3 scatter.104
  452.8 3.8 while.247
  456.7 2.2 scatter.105
  459.1 2.2 scatter.106
  461.3 1.6 constant_dynamic-slice_fusion.7
  462.9 10.7 %while.255 = (s32[]{:T(128)}, f32[6,16,16]{1,0,2:T(8,128)S(1)}, s32[]{:T(128)}) while((s32[]{:T(128)}, f32[6,16,16]{1,0,2:T(8,128)S(1)}, s32[]{:T(128)}) %tuple.622), condition=%wide.region_31.32_spmd.clone.clone, body=%wide.region_30.31_spmd.clone.clone.sunk | while | flops 5186 | bytes 28397 | solution.py:38
  473.6 2.2 scatter.109
  475.8 0.9 copy.164
  (1779 shorter events, 111.6 us)
Async XLA Ops:
  7.2 3.8 copy-start.2
  7.2 4.0 copy-start.1
  7.2 24.3 %all-gather.5.cloned.1.call-start = ((), (), s32[]{:S(2)}) async-start(), calls=%async_computation.1 | async-start | bytes 4718592 | tf_op jit(solution)/shard_map/all_gather | solution.py:97
  11.0 91.5 %all-gather.3.cloned.1.call-start = ((), (), s32[]{:S(2)}) async-start(), calls=%async_computation | async-start | bytes 7864320 | tf_op jit(solution)/shard_map/all_gather | solution.py:101
  12.6 268.2 %all-reduce.2.cloned.1.call-start = ((), (), s32[]{:S(2)}) async-start(), calls=%async_computation.2 | async-start | bytes 9437184 | tf_op jit(solution)/shard_map/psum | solution.py:107
  112.2 0.7 copy-start.3
  285.2 2.7 copy-start
Sparse Core Ops, SparseCore 0:
  11.1 20.3 all-gather.4
  33.3 69.1 all-gather.2
  112.3 168.4 all-reduce.1
where the time goes:
time: 485 us; the launch traced here: 483 us
  waiting for transfers between devices  257 us (53%)
  local copies, waits for them, and re-layouts  128 us (26%)
  other arithmetic  55.7 us (11%)
  between operations  14.5 us (3%)
  matrix products  13.4 us (3%)
  loops' own time  11.6 us (2%)
    psum x1, waiting for transfers between devices, shards(): total = lax.psum(update, 'layer')  167 us
    all_gather x1, waiting for transfers between devices, shards(): lax.all_gather(left_masked, 'col', axis=2, tiled=True)  71 us
    scatter x7, local copies, waits for them, and re-layouts, factor(): current = current.at[:, end:, end:].set(trailing)  23.7 us
    dynamic_slice x128, local copies, waits for them, and re-layouts, eliminate_sweep(): pivot = current[:, step, step]  23.6 us
    scatter x7, local copies, waits for them, and re-layouts, factor(): current = current.at[:, offset:end, end:].set(strip)  22.9 us
    while x224, local copies, waits for them, and re-layouts  22 us
    all_gather x1, waiting for transfers between devices, shards(): right_full = lax.all_gather(right_masked, 'row', axis=1, tiled=True)  18.9 us
    scatter x8, local copies, waits for them, and re-layouts, factor(): current = current.at[:, offset:, offset:end].set(panel)  16 us
  transfers between devices with their start and end apart: 3, of which 3 were waited for; matrix products, arithmetic and copies ran while one was open for 1% of the time, Pallas kernels for 0%

commit v1 on v0

v1 whole, which is shorter than its diff:
```python
import jax
import jax.numpy as jnp
from jax import lax
from jax.experimental import pallas as pl
from jax.experimental.pallas import tpu as pltpu
from jax.sharding import PartitionSpec as P

BLK = 128
SEGMENTS = 4


def lu_blocks(ref, count):
    lanes = lax.broadcasted_iota(jnp.int32, (1, BLK), 1)
    span = BLK // SEGMENTS
    for segment in range(SEGMENTS):
        top = segment * span
        height = BLK - top
        rows = top + lax.broadcasted_iota(jnp.int32, (height, 1), 0)

        def panel(index, carry):
            first = top + index * 8
            for j in range(8):
                keep = jnp.logical_and(lanes > j, lanes + first < BLK)
                below = rows > first + j
                for b in range(count):
                    row = ref[b, pl.ds(first + j, 1), :]
                    inverse = 1.0 / row[:, j : j + 1]
                    current = ref[b, top:, :]
                    factors = jnp.where(below, current[:, j : j + 1] * inverse, 0.0)
                    updated = current - factors * jnp.where(keep, row, 0.0)
                    placed = jnp.logical_and(below, lanes == j)
                    ref[b, top:, :] = jnp.where(placed, factors, updated)
            for b in range(count):
                ref[b] = pltpu.roll(ref[b], BLK - 8, 1)
            return carry

        lax.fori_loop(0, span // 8, panel, 0)


def lu_kernel(blocks_ref, out_ref):
    out_ref[...] = blocks_ref[...]
    lu_blocks(out_ref, out_ref.shape[0])


def factor(blocks):
    return pl.pallas_call(
        lu_kernel,
        out_shape=jax.ShapeDtypeStruct(blocks.shape, jnp.float32),
        in_specs=[pl.BlockSpec(memory_space=pltpu.VMEM)],
        out_specs=pl.BlockSpec(memory_space=pltpu.VMEM),
    )(blocks)


def mask_rows(panel, pattern, block):
    count, length, inner = panel.shape
    shaped = panel.reshape(count, length // block, block, inner)
    return (shaped * pattern[:, :, None, None].astype(panel.dtype)).reshape(count, length, inner)


def mask_cols(panel, pattern, block):
    count, inner, length = panel.shape
    shaped = panel.reshape(count, inner, length // block, block)
    return (shaped * pattern[:, None, :, None].astype(panel.dtype)).reshape(count, inner, length)


def diagonal(matrix):
    width = matrix.shape[1]
    per_group = lax.axis_size("col") // lax.axis_size("row")
    column = lax.axis_index("col")
    valid = column // per_group == lax.axis_index("row")
    square = lax.dynamic_slice_in_dim(matrix, column % per_group * width, width, 0)
    blocks = jnp.stack(
        [square[j * BLK : (j + 1) * BLK, j * BLK : (j + 1) * BLK] for j in range(width // BLK)]
    )
    return jnp.where(valid, blocks, 0.0)


def shards(lpanel, upanel, lpat, upat, ancestor_entries):
    left_masked = mask_rows(lpanel[0], lpat[0], BLK)
    right_masked = mask_cols(upanel[0], upat[0], BLK)
    right_full = lax.all_gather(right_masked, "row", axis=1, tiled=True)
    update = jnp.einsum(
        "kmw,kwn->mn",
        lax.all_gather(left_masked, "col", axis=2, tiled=True),
        right_full,
        preferred_element_type=jnp.float32,
    )
    share_rows = update.shape[0] // lax.axis_size("layer")
    offset = lax.axis_index("layer") * share_rows
    first = lax.axis_index("layer") == 0
    pivots = jnp.where(first, diagonal(ancestor_entries), 0.0) - diagonal(update)
    diag_lu = factor(lax.psum(pivots, ("layer", "row")))
    total = lax.psum_scatter(update, "layer", scatter_dimension=0, tiled=True)
    schur = lax.dynamic_slice_in_dim(ancestor_entries, offset, share_rows, 0) - total
    return (schur, diag_lu)


def solution(mesh):
    return jax.shard_map(
        shards,
        mesh=mesh,
        in_specs=(
            P("layer", None, "row", "col"),
            P("layer", None, "row", "col"),
            P("layer", None, "row"),
            P("layer", None, "col"),
            P("row", "col"),
        ),
        out_specs=(P(("row", "layer"), "col"), P("col", None, None)),
        check_vma=False,
    )
```

time: 485 us -> 541 us (1.12)
  waiting for transfers between devices: 257 us -> 428 us
  local copies, waits for them, and re-layouts: 128 us -> 11.4 us
  Pallas kernels: 0 us -> 70.9 us
  other arithmetic: 55.7 us -> 6.48 us
  loops' own time: 11.6 us -> 0 us
    reduce_scatter x0 -> x1, waiting for transfers between devices: none -> 159 us  [shards(): total = lax.psum_scatter(update, 'layer', scatter_dimension=0, tiled=True)]
    pallas_call x0 -> x1, Pallas kernels: none -> 70.9 us  [factor(): pl.pallas_call(lu_kernel, out_shape=jax.ShapeDtypeStruct(blocks.shape, jn...]
    scatter x22 -> x0, local copies, waits for them, and re-layouts: 62.5 us -> none  [the longest x7 23.7 us: factor(): current = current.at[:, end:, end:].set(trailing)]
    dynamic_slice x226 -> x0, local copies, waits for them, and re-layouts: 26.2 us -> none  [the longest x128 23.6 us: eliminate_sweep(): pivot = current[:, step, step]]
    while x239 -> x0, local copies, waits for them, and re-layouts: 22.9 us -> none
    psum x1, waiting for transfers between devices: 167 us -> 183 us  [shards(): diag_lu = factor(lax.psum(pivots, ('layer', 'row')))]
    mul x160 -> x0, local copies, waits for them, and re-layouts: 12.2 us -> none  [the longest x128 10.7 us: eliminate_sweep(): current = current - column[:, :, None] * row_part[:, None, :]]
    select_n x128 -> x0, other arithmetic: 11.7 us -> none  [eliminate_sweep(): return jnp.where(placed, column[:, :, None], current)]
  transfers between devices with their start and end apart: 3 -> 4, of which waited for: 3 -> 4; matrix products, arithmetic and copies ran while one was open for 1% -> 1% of each run, Pallas kernels for 0% -> 13%
where the time goes in v1:
time: 541 us; the launch traced here: 540 us
  waiting for transfers between devices  428 us (79%)
  Pallas kernels  70.9 us (13%)
  between operations  13.8 us (3%)
  local copies, waits for them, and re-layouts  11.4 us (2%)
  matrix products  9.68 us (2%)
  other arithmetic  6.48 us (1%)
    psum x1, waiting for transfers between devices, shards(): diag_lu = factor(lax.psum(pivots, ('layer', 'row')))  183 us
    reduce_scatter x1, waiting for transfers between devices, shards(): total = lax.psum_scatter(update, 'layer', scatter_dimension=0, tiled=True)  159 us
    all_gather x1, waiting for transfers between devices, shards(): lax.all_gather(left_masked, 'col', axis=2, tiled=True)  71 us
    pallas_call x1, Pallas kernels, factor(): pl.pallas_call(lu_kernel, out_shape=jax.ShapeDtypeStruct(blocks.shape, jn...  70.9 us
    all_gather x1, waiting for transfers between devices, shards(): right_full = lax.all_gather(right_masked, 'row', axis=1, tiled=True)  13.8 us
  transfers between devices with their start and end apart: 4, of which 4 were waited for; matrix products, arithmetic and copies ran while one was open for 1% of the time, Pallas kernels for 13%

profile of v1, /device:TPU:2, one launch (start us, length us, event | category | flops | bytes accessed | tf_op | source)
XLA Modules:
  0.0 540.4 jit_solution(5814518375085656059)
XLA Ops:
  7.2 0.0 copy-start.1
  7.2 0.0 copy-start
  7.2 0.0 all-gather.5.cloned.1.call-start
  7.2 0.9 copy.8
  8.1 0.1 copy.9
  8.2 0.1 broadcast_bitcast_fusion.1
  8.3 2.7 bitcast_multiply_fusion
  10.9 0.0 all-gather.5.cloned.1.call-update
  11.0 0.0 all-gather.3.cloned.1.call-start
  11.0 0.0 copy-done.1
  11.0 0.1 copy.7
  11.1 0.1 broadcast_bitcast_fusion
  11.2 0.0 copy-done
  11.2 1.4 bitcast_multiply_fusion.1
  12.6 0.0 all-gather.3.cloned.1.call-update
  12.6 0.0 all-reduce.2.cloned.1.call-start
  12.7 0.8 fusion.11
  13.5 0.8 fusion.10
  14.4 0.8 fusion.9
  15.2 0.8 fusion.8
  16.1 0.8 fusion.7
  16.9 0.8 fusion.6
  17.8 13.8 %all-gather.5.cloned.1.call-done = bf16[8,256,768]{2,1,0:T(8,128)(2,1)} async-done(((bf16[8,128,768]{2,1,0:T(8,128)(2,1)}), bf16[8,256,768]{2,1,0:T(8,128)(2,1)}) %all-gather.5.cloned.1.call-update) | async-done | bytes 3145744 | tf_op jit(solution)/shard_map/all_gather | solution.py:81
  31.5 71.0 %all-gather.3.cloned.1.call-done = bf16[8,1536,256]{1,2,0:T(8,128)(2,1)} async-done(((bf16[8,1536,64]{1,2,0:T(8,128)(2,1)}), bf16[8,1536,256]{1,2,0:T(8,128)(2,1)}) %all-gather.3.cloned.1.call-update) | async-done | bytes 6291472 | tf_op jit(solution)/shard_map/all_gather | solution.py:84
  102.5 9.7 %convolution_bitcast_fusion = f32[1536,768]{1,0:T(8,128)} fusion(bf16[8,1536,256]{1,2,0:T(8,128)(2,1)} %all-gather.3.cloned.1.call-done, bf16[8,256,768]{2,1,0:T(8,128)(2,1)} %all-gather.5.cloned.1.call-done), kind=kOutput, calls=%fused_computation | convolution fusion | flops 4831838208 | bytes 14155776 | tf_op jit(solution)/shard_map/kmw,kwn->mn/dot_general | solution.py:82
  112.2 0.8 fusion.5
  113.0 0.8 fusion.4
  113.9 0.8 fusion.3
  114.7 0.8 fusion.2
  115.6 0.8 fusion.1
  116.4 0.8 fusion
  117.2 0.8 select_subtract_fusion
  118.1 0.0 all-reduce.2.cloned.1.call-update
  118.1 0.0 reduce-scatter.2.cloned.1.call-start
  118.1 0.5 reduce-scatter.2.cloned.1.call-update
  118.7 183.2 %all-reduce.2.cloned.1.call-done.blocks_ref = f32[6,128,128]{2,1,0:T(8,128)} async-done(((f32[6,128,128]{2,1,0:T(8,128)}), f32[6,128,128]{2,1,0:T(8,128)}) %all-reduce.2.cloned.1.call-update) | async-done | bytes 393232 | tf_op jit(solution)/shard_map/psum | solution.py:92
  301.9 70.9 %shard_map.68 = f32[6,128,128]{2,1,0:T(8,128)} custom-call(f32[6,128,128]{2,1,0:T(8,128)} %all-reduce.2.cloned.1.call-done.blocks_ref), custom_call_target="tpu_custom_call" | custom-call | tf_op jit(solution)/shard_map/pallas_call | solution.py:46
  372.8 159.4 %reduce-scatter.2.cloned.1.call-done = f32[48,768]{1,0:T(8,128)} async-done(((f32[1536,768]{1,0:T(8,128)}), f32[48,768]{1,0:T(8,128)}) %reduce-scatter.2.cloned.1.call-update) | async-done | bytes 147472 | tf_op jit(solution)/shard_map/reduce_scatter | solution.py:93
  532.2 1.7 dynamic-slice_subtract_fusion
  (2 shorter events, 0.0 us)
Async XLA Ops:
  7.2 3.8 copy-start.1
  7.2 4.0 copy-start
  7.2 24.3 %all-gather.5.cloned.1.call-start = ((), (), s32[]{:S(2)}) async-start(), calls=%async_computation.2 | async-start | bytes 4718592 | tf_op jit(solution)/shard_map/all_gather | solution.py:81
  11.0 91.5 %all-gather.3.cloned.1.call-start = ((), (), s32[]{:S(2)}) async-start(), calls=%async_computation.1 | async-start | bytes 7864320 | tf_op jit(solution)/shard_map/all_gather | solution.py:84
  12.6 289.3 %all-reduce.2.cloned.1.call-start = ((), (), s32[]{:S(2)}) async-start(), calls=%async_computation.4 | async-start | bytes 786432 | tf_op jit(solution)/shard_map/psum | solution.py:92
  118.1 414.1 %reduce-scatter.2.cloned.1.call-start = ((), (), s32[]{:S(2)}) async-start(), calls=%async_computation.3 | async-start | bytes 4866048 | tf_op jit(solution)/shard_map/reduce_scatter | solution.py:93
Sparse Core Ops, SparseCore 0:
  11.1 20.3 all-gather.4
  33.3 69.1 all-gather.2
  118.2 183.6 all-reduce.1
  305.7 226.4 reduce-scatter.1

commit v2 on v1

v2 whole, which is shorter than its diff:
```python
import functools

import jax
import jax.numpy as jnp
from jax import lax
from jax.experimental import pallas as pl
from jax.experimental.pallas import tpu as pltpu
from jax.sharding import PartitionSpec as P

MESH = pl.DeviceIdType.MESH
BLK = 128
SEGMENTS = 4
NX, NY, NZ = 4, 4, 8
SUPER = 8
PIECE = 64
ROWS = 1536
COLS = 768
HALF = COLS // 2
GROUP = 16
PARTS = 3
CHUNKS = NY * PARTS
HEIGHT = NZ * GROUP
STRIP = NZ * GROUP * PARTS


def lu_blocks(ref, count):
    lanes = lax.broadcasted_iota(jnp.int32, (8, BLK), 1)
    subs = lax.broadcasted_iota(jnp.int32, (8, BLK), 0)
    lane = lax.broadcasted_iota(jnp.int32, (1, BLK), 1)
    tiles_all = BLK // 8
    per_segment = tiles_all // SEGMENTS
    for segment in range(SEGMENTS):
        top = segment * per_segment

        def panel(index, carry):
            place = top + index
            first = place * 8
            tops = [ref[b, pl.ds(pl.multiple_of(first, 8), 8), :] for b in range(count)]
            rows = [[] for _ in range(count)]
            scales = [jnp.ones((1, BLK), jnp.float32) for _ in range(count)]
            for j in range(8):
                keep = jnp.logical_and(lane > j, lane + first < BLK)
                for b in range(count):
                    row = tops[b][j : j + 1, :]
                    inverse = 1.0 / row[:, j : j + 1]
                    scaled = jnp.where(keep, row * inverse, 0.0)
                    rows[b].append(scaled)
                    scales[b] = jnp.where(lane == j, inverse, scales[b])
                    column = jnp.where(subs > j, tops[b][:, j : j + 1], 0.0)
                    tops[b] = tops[b] - column * scaled
            for b in range(count):
                lower = jnp.logical_and(subs > lanes, lanes < 8)
                done = jnp.where(lower, tops[b] * scales[b], tops[b])
                ref[b, pl.ds(pl.multiple_of(first, 8), 8), :] = pltpu.roll(done, first, 1)
            for b in range(count):
                for tile in range(top + 1, tiles_all):
                    old = ref[b, tile * 8 : tile * 8 + 8, :]
                    new = old
                    for j in range(8):
                        new = new - new[:, j : j + 1] * rows[b][j]
                    new = pltpu.roll(new * scales[b], BLK - 8, 1)
                    ref[b, tile * 8 : tile * 8 + 8, :] = jnp.where(tile > place, new, old)
            return carry

        lax.fori_loop(0, per_segment, panel, 0)


def kernel(
    l_hbm, r_hbm, lpat, upat, anc_hbm, schur_ref, diag_ref,
    lin, rin, anc, lbuf, rbuf, pbuf, ya, yb, yp, ym, zbuf, zp, zm, sbuf, dbuf,
    hsem, xs, xr, rsend, rrecv, ysend, yrecv, zsend, zrecv, dsend, drecv,
):
    layer, c, x = lax.axis_index("layer"), lax.axis_index("row"), lax.axis_index("col")
    y, z = layer // NZ, layer % NZ
    right, left = (x + 1) % NX, (x + NX - 1) % NX
    up, down = (y + 1) % NY * NZ + z, (y + NY - 1) % NY * NZ + z
    ahead, behind = y * NZ + (z + 1) % NZ, y * NZ + (z + NZ - 1) % NZ

    def strip_of(order):
        return (y + 2 - order - order // 2 + 2 * (order // 3) + NY) % NY

    def remote(src, dst, send, recv, device):
        return pltpu.make_async_remote_copy(
            src_ref=src, dst_ref=dst, send_sem=send, recv_sem=recv, device_id=device, device_id_type=MESH
        )

    def load_left(order):
        strip = strip_of(order)
        return pltpu.make_async_copy(
            l_hbm.at[:, :, pl.ds(pl.multiple_of(strip * STRIP, BLK), STRIP)], lin.at[order], hsem.at[order]
        )

    load_right = pltpu.make_async_copy(r_hbm, rin, hsem.at[4])
    load_anc = pltpu.make_async_copy(anc_hbm.at[pl.ds(pl.multiple_of(layer * 48, 8), 48), :], anc, hsem.at[5])

    def xcopy(kind, t):
        b, s = strip_of(t % NY), t // NY
        if kind == 0:
            src, dst, to = lbuf.at[0, b, s], lbuf.at[1, b, s], right
        elif kind == 1:
            src, dst, to = lbuf.at[0, b, s], lbuf.at[2, b, s], left
        elif kind == 2:
            src, dst, to = lbuf.at[1, b, s, 0:4], lbuf.at[3, b, s, 0:4], right
        else:
            src, dst, to = lbuf.at[2, b, s, 4:8], lbuf.at[3, b, s, 4:8], left
        return remote(src, dst, xs.at[kind, t], xr.at[kind, t], {"col": to})

    def rcopy(h, core):
        return remote(rbuf.at[2 * core + h], rbuf.at[2 * core + h], rsend.at[h], rrecv.at[h], {"row": 1 - c})

    def ycopy(kind, s):
        if kind == 0:
            src, dst, to = pbuf.at[4 * s, :, 0:HALF], ya.at[s], up
        elif kind == 1:
            src, dst, to = pbuf.at[4 * s, :, HALF:COLS], yb.at[s], down
        elif kind == 2:
            src, dst, to = pbuf.at[4 * s + 1], yp.at[s], up
        else:
            src, dst, to = pbuf.at[4 * s + 2], ym.at[s], down
        return remote(src, dst, ysend.at[kind, s], yrecv.at[kind, s], {"layer": to})

    def zcopy(way, s, h):
        if way == 0:
            block, to, landing = (z + 4 - h) % NZ, ahead, zp
            cut = pl.ds(HALF, HALF)
        else:
            block, to, landing = (z + 4 + h) % NZ, behind, zm
            cut = pl.ds(0, HALF)
        if h == 0:
            src, dst = zbuf.at[s, block, :, cut], landing.at[4 * s, :, cut]
        else:
            src, dst = zbuf.at[s, block], landing.at[4 * s + h]
        return remote(src, dst, zsend.at[way, 4 * s + h], zrecv.at[way, 4 * s + h], {"layer": to})

    load_left(0).start()
    load_right.start()
    for order in range(1, NY):
        load_left(order).start()
    load_anc.start()
    barrier = pltpu.get_barrier_semaphore()
    for to in (left, right):
        pl.semaphore_signal(barrier, inc=1, device_id={"col": to}, device_id_type=MESH)
    own = c * (NY * NZ) + layer
    members = 2 * NY * NZ

    def greet(i, carry):
        to = (own + i) % members
        pl.semaphore_signal(
            barrier, inc=1, device_id={"layer": to % (NY * NZ), "row": to // (NY * NZ)}, device_id_type=MESH
        )
        return carry

    lax.fori_loop(1, members, greet, 0)

    def prepare_left(order):
        b = strip_of(order)
        load_left(order).wait()
        for j in range(STRIP // BLK):
            pieces = []
            for k in range(SUPER):
                tile = lin[order, k, :, j * BLK : (j + 1) * BLK]
                pieces.append(jnp.where(lpat[k, 3 * b + j] > 0, tile, jnp.zeros_like(tile)))
            turned = jnp.concatenate(pieces, axis=0).T
            for g in range(8):
                place = 8 * j + g
                lbuf[0, b, place % PARTS, place // PARTS] = turned[g * GROUP : (g + 1) * GROUP, :]

    prepare_left(0)
    pl.semaphore_wait(barrier, members + 1)
    xcopy(0, 0).start()
    xcopy(1, 0).start()
    load_right.wait()
    for k in range(SUPER):
        for j in range(COLS // BLK):
            for h in range(2):
                tile = rin[k, h * PIECE : (h + 1) * PIECE, j * BLK : (j + 1) * BLK]
                rbuf[2 * c + h, k * PIECE : (k + 1) * PIECE, j * BLK : (j + 1) * BLK] = jnp.where(
                    upat[j, k] > 0, tile, jnp.zeros_like(tile)
                )
    for h in range(2):
        rcopy(h, c).start()
    for order in range(1, NY):
        prepare_left(order)
        xcopy(0, order).start()
        xcopy(1, order).start()
    for h in range(2):
        rcopy(h, 1 - c).wait_recv()
    load_anc.wait()

    owner = jnp.logical_and(c == x // 2, y // 2 == x % 2)

    def step(t, carry):
        @pl.when(t < CHUNKS)
        def _():
            xcopy(0, t).wait_recv()
            xcopy(2, t).start()
            xcopy(1, t).wait_recv()
            xcopy(3, t).start()

        @pl.when(t < CHUNKS - NY)
        def _():
            xcopy(0, t + NY).start()
            xcopy(1, t + NY).start()

        @pl.when(jnp.logical_and(t >= 1, t < CHUNKS + 1))
        def _():
            u = t - 1
            xcopy(2, u).wait_recv()
            xcopy(3, u).wait_recv()
            b, s = strip_of(u % NY), u // NY
            for n in range(COLS // 256):
                total = None
                for slot, shift in enumerate((0, 3, 1, 2)):
                    product = jnp.dot(
                        lbuf[slot, b, s].reshape(HEIGHT, SUPER * PIECE),
                        rbuf[(x + shift) % NX, :, n * 256 : (n + 1) * 256],
                        preferred_element_type=jnp.float32,
                    )
                    total = product if total is None else total + product
                pbuf[u, :, n * 256 : (n + 1) * 256] = total

            @pl.when(u % NY == 0)
            def _():
                ycopy(0, s).start()
                ycopy(1, s).start()

        @pl.when(jnp.logical_and(t >= 2, t < CHUNKS + 2))
        def _():
            v = t - 2
            s = v // NY

            @pl.when(v % NY == 1)
            def _():
                ycopy(0, s).wait_recv()
                pbuf[v, :, 0:HALF] = pbuf[v, :, 0:HALF] + ya[s]
                ycopy(2, s).start()

            @pl.when(v % NY == 2)
            def _():
                ycopy(1, s).wait_recv()
                pbuf[v, :, HALF:COLS] = pbuf[v, :, HALF:COLS] + yb[s]
                ycopy(3, s).start()

        @pl.when(jnp.logical_and(t >= 11, t % 4 == 3))
        def _():
            s = (t - 11) // 4
            for way in range(2):
                zcopy(way, s, 3).wait_recv()
            total = zbuf[s, z] + zp[4 * s + 3] + zm[4 * s + 3]
            rows = pl.ds(pl.multiple_of(GROUP * s, GROUP), GROUP)
            final = anc[rows, :] - total
            sbuf[s] = final
            schur_ref[rows, :] = final

            @pl.when(owner)
            def _():
                place = STRIP * (y % 2) + 48 * z + GROUP * s
                j = place // BLK
                cut = pl.ds(pl.multiple_of(j * BLK, BLK), BLK)
                spot = pl.ds(pl.multiple_of(place, GROUP), GROUP)
                dbuf[spot, :] = sbuf[s, :, cut]

                def hand_out(i, carry):
                    to = (own + i) % members
                    remote(
                        sbuf.at[s, :, cut], dbuf.at[spot, :], dsend.at[s], drecv.at[0],
                        {"layer": to % (NY * NZ), "row": to // (NY * NZ)},
                    ).start()
                    return carry

                lax.fori_loop(1, members, hand_out, 0)

        @pl.when(jnp.logical_and(t >= 7, t < 19))
        def _():
            s, h_now = (t - 7) // 4, (t - 7) % 4
            for h in range(4):

                @pl.when(h_now == h)
                def _():
                    if h == 0:
                        ycopy(2, s).wait_recv()
                        ycopy(3, s).wait_recv()
                        zbuf[s] = (pbuf[4 * s + 3] + yp[s] + ym[s]).reshape(NZ, GROUP, COLS)
                    for way in range(2):
                        block = (z + 4 - h) % NZ if way == 0 else (z + 4 + h) % NZ
                        landing = zp if way == 0 else zm
                        cut = slice(HALF, COLS) if way == 0 else slice(0, HALF)
                        if h == 1:
                            zcopy(way, s, 0).wait_recv()
                            zbuf[s, block, :, cut] = zbuf[s, block, :, cut] + landing[4 * s, :, cut]
                        elif h > 1:
                            zcopy(way, s, h - 1).wait_recv()
                            zbuf[s, block] = zbuf[s, block] + landing[4 * s + h - 1]
                        zcopy(way, s, h).start()

        return carry

    lax.fori_loop(0, 20, step, 0)

    @pl.when(owner)
    def _():
        pltpu.make_async_copy(dbuf.at[0:720], dbuf.at[0:720], drecv.at[0]).wait()

    @pl.when(jnp.logical_not(owner))
    def _():
        pltpu.make_async_copy(dbuf, dbuf, drecv.at[0]).wait()

    diag_ref[...] = dbuf[...].reshape(6, BLK, BLK)
    lu_blocks(diag_ref, 6)

    @pl.when(owner)
    def _():
        for s in range(PARTS):
            sent = pbuf.at[0:7, 0:24, :]
            pltpu.make_async_copy(sent, sent, dsend.at[s]).wait()

    for h in range(2):
        rcopy(h, c).wait_send()

    def drain_x(t, carry):
        for kind in range(4):
            xcopy(kind, t).wait_send()
        return carry

    lax.fori_loop(0, CHUNKS, drain_x, 0)

    def drain_yz(s, carry):
        for kind in range(4):
            ycopy(kind, s).wait_send()
        for h in range(4):
            for way in range(2):
                zcopy(way, s, h).wait_send()
        return carry

    lax.fori_loop(0, PARTS, drain_yz, 0)


def shards(lpanel, upanel, lpat, upat, ancestor_entries):
    f32, bf16 = jnp.float32, jnp.bfloat16
    vmem = pl.BlockSpec(memory_space=pltpu.VMEM)
    smem = pl.BlockSpec(memory_space=pltpu.SMEM)
    anywhere = pl.BlockSpec(memory_space=pl.ANY)
    dma = pltpu.SemaphoreType.DMA
    return pl.pallas_call(
        kernel,
        out_shape=(jax.ShapeDtypeStruct((48, COLS), f32), jax.ShapeDtypeStruct((6, BLK, BLK), f32)),
        in_specs=[anywhere, anywhere, smem, smem, anywhere],
        out_specs=(vmem, vmem),
        scratch_shapes=[
            pltpu.VMEM((NY, SUPER, PIECE, STRIP), bf16),
            pltpu.VMEM((SUPER, 2 * PIECE, COLS), bf16),
            pltpu.VMEM((48, COLS), f32),
            pltpu.VMEM((NX, NY, PARTS, NZ, GROUP, SUPER * PIECE), bf16),
            pltpu.VMEM((NX, SUPER * PIECE, COLS), bf16),
            pltpu.VMEM((CHUNKS, HEIGHT, COLS), f32),
            pltpu.VMEM((PARTS, HEIGHT, HALF), f32),
            pltpu.VMEM((PARTS, HEIGHT, HALF), f32),
            pltpu.VMEM((PARTS, HEIGHT, COLS), f32),
            pltpu.VMEM((PARTS, HEIGHT, COLS), f32),
            pltpu.VMEM((PARTS, NZ, GROUP, COLS), f32),
            pltpu.VMEM((4 * PARTS, GROUP, COLS), f32),
            pltpu.VMEM((4 * PARTS, GROUP, COLS), f32),
            pltpu.VMEM((PARTS, GROUP, COLS), f32),
            pltpu.VMEM((6 * BLK, BLK), f32),
            dma((6,)), dma((4, CHUNKS)), dma((4, CHUNKS)), dma((2,)), dma((2,)),
            dma((4, PARTS)), dma((4, PARTS)), dma((2, 4 * PARTS)), dma((2, 4 * PARTS)), dma((PARTS,)), dma((1,)),
        ],
        compiler_params=pltpu.CompilerParams(
            collective_id=0, has_side_effects=True, vmem_limit_bytes=60 * 1024 * 1024
        ),
    )(
        jnp.swapaxes(lpanel[0], 1, 2),
        upanel[0],
        lpat[0],
        jnp.swapaxes(upat[0], 0, 1),
        ancestor_entries,
    )


def solution(mesh):
    return jax.shard_map(
        shards,
        mesh=mesh,
        in_specs=(
            P("layer", None, "row", "col"),
            P("layer", None, "row", "col"),
            P("layer", None, "row"),
            P("layer", None, "col"),
            P("row", "col"),
        ),
        out_specs=(P(("row", "layer"), "col"), P("col", None, None)),
        check_vma=False,
    )
```

time: 541 us -> 152 us (0.28)
  waiting for transfers between devices: 428 us -> 0 us
  Pallas kernels: 70.9 us -> 145 us
  between operations: 13.8 us -> 0.64 us
  matrix products: 9.68 us -> 0 us
  local copies, waits for them, and re-layouts: 11.4 us -> 4.62 us
  other arithmetic: 6.48 us -> 0 us
    psum x1 -> x0, waiting for transfers between devices: 183 us -> none  [shards(): diag_lu = factor(lax.psum(pivots, ('layer', 'row')))]
    reduce_scatter x1 -> x0, waiting for transfers between devices: 159 us -> none  [shards(): total = lax.psum_scatter(update, 'layer', scatter_dimension=0, tiled=True)]
    all_gather x2 -> x0, waiting for transfers between devices: 84.7 us -> none  [the longest x1 71 us: shards(): lax.all_gather(left_masked, 'col', axis=2, tiled=True)]
    pallas_call x1, Pallas kernels: 70.9 us -> 145 us  [shards(): pl.pallas_call(kernel, out_shape=(jax.ShapeDtypeStruct((48, COLS), f32),...]
    dot_general x1 -> x0, matrix products: 9.68 us -> none  [shards(): jnp.einsum('kmw,kwn->mn', lax.all_gather(left_masked, 'col', axis=2, tile...]
    unnamed x15 -> x2, local copies, waits for them, and re-layouts: 9.34 us -> 3.35 us
  transfers between devices with their start and end apart: 4 -> 0, of which waited for: 4 -> 0; matrix products, arithmetic and copies ran while one was open for 1% -> 0% of each run, Pallas kernels for 13% -> 0%
where the time goes in v2:
time: 152 us; the launch traced here: 151 us
  Pallas kernels  145 us (95%)
  local copies, waits for them, and re-layouts  4.62 us (3%)
    pallas_call x1, Pallas kernels, shards(): pl.pallas_call(kernel, out_shape=(jax.ShapeDtypeStruct((48, COLS), f32),...  145 us
    unnamed x2, local copies, waits for them, and re-layouts  3.35 us

profile of v2, /device:TPU:2, one launch (start us, length us, event | category | flops | bytes accessed | tf_op | source)
XLA Modules:
  0.0 150.5 jit_solution(17658278455110193383)
XLA Ops:
  0.6 1.3 copy.11
  1.9 145.2 %shard_map.68 = (f32[48,768]{1,0:T(8,128)}, f32[6,128,128]{2,1,0:T(8,128)}) custom-call(bf16[8,64,1536]{2,1,0:T(8,128)(2,1)} %bitcast.11, bf16[8,128,768]{2,1,0:T(8,128)(2,1)} %bitcast.12, s32[8,12]{1,0:T(8,128)} %bitcast.14, s32[6,8]{1,0:T(8,128)} %bitcast.13, f32[1536,768]{1,0:T(8,128)} %anc_hbm.1), custom_call_target="tpu_custom_call" | custom-call | tf_op jit(solution)/shard_map/pallas_call | solution.py:344
  147.2 1.6 %copy.14 = f32[48,768]{1,0:T(8,128)} copy(f32[48,768]{1,0:T(8,128)} %get-tuple-element.4) | data formatting | bytes 294912
  148.7 1.8 %copy.15 = f32[6,128,128]{2,1,0:T(8,128)} copy(f32[6,128,128]{2,1,0:T(8,128)} %get-tuple-element.5) | data formatting | bytes 786432

commit v3 on v2

v3 whole, which is shorter than its diff:
```python
import jax
import jax.numpy as jnp
from jax import lax
from jax.experimental import pallas as pl
from jax.experimental.pallas import tpu as pltpu
from jax.sharding import PartitionSpec as P

MESH = pl.DeviceIdType.MESH
BLK = 128
SEGMENTS = 4
NX, NY, NZ = 4, 4, 8
SUPER = 8
PIECE = 64
ROWS = 1536
COLS = 768
HALF = COLS // 2
GROUP = 16
PARTS = 3
CHUNKS = NY * PARTS
HEIGHT = NZ * GROUP
STRIP = NZ * GROUP * PARTS
LEAD = 3
START = 10


def lu_segment(segment, work, out):
    count = out.shape[0]
    lanes = lax.broadcasted_iota(jnp.int32, (8, BLK), 1)
    subs = lax.broadcasted_iota(jnp.int32, (8, BLK), 0)
    total = BLK // 8
    per_segment = total // SEGMENTS
    live = total - segment * per_segment

    def spread(line):
        return jnp.broadcast_to(line, (8, BLK))

    def panel(index, carry):
        first = (segment * per_segment + index) * 8
        tops = [work[b, 0:8, :] for b in range(count)]
        rest = [[work[b, t * 8 : t * 8 + 8, :] for t in range(1, live)] for b in range(count)]
        scales = [jnp.ones((8, BLK), jnp.float32) for _ in range(count)]
        columns = [[spread(tops[b][:, j : j + 1]) for j in range(8)] for b in range(count)]
        for j in range(8):
            keep = jnp.logical_and(lanes > j, lanes + first < BLK)
            for b in range(count):
                inverse = 1.0 / spread(columns[b][j][j : j + 1, :])
                scaled = jnp.where(keep, spread(tops[b][j : j + 1, :]), 0.0) * inverse
                scales[b] = jnp.where(lanes == j, inverse, scales[b])
                below = jnp.where(subs > j, columns[b][j], 0.0)
                tops[b] = tops[b] - below * scaled
                for q in range(j + 1, 8):
                    columns[b][q] = columns[b][q] - below * (spread(columns[b][q][j : j + 1, :]) * inverse)
                for i in range(live - 1):
                    rest[b][i] = rest[b][i] - rest[b][i][:, j : j + 1] * scaled
        lower = jnp.logical_and(subs > lanes, lanes < 8)
        for b in range(count):
            done = jnp.where(lower, tops[b] * scales[b], tops[b])
            out[b, pl.ds(pl.multiple_of(first, 8), 8), :] = pltpu.roll(done, first, 1)
            for i in range(live - 1):
                work[b, i * 8 : i * 8 + 8, :] = pltpu.roll(rest[b][i] * scales[b], BLK - 8, 1)
        return carry

    lax.fori_loop(0, per_segment, panel, 0)


def finish_kernel(schur_ref, part_ref, rest_ref, schur_out, out, work):
    schur_out[...] = schur_ref[...]
    out[...] = part_ref[...]
    work[...] = rest_ref[...]
    lu_segment(SEGMENTS - 1, work, out)


def kernel(
    l_hbm, r_hbm, lpat, upat, anc_hbm, schur_ref, part_ref, rest_ref,
    lin, rin, anc, ancd, lbuf, rbuf, pbuf, ya, yb, yp, ym, zbuf, zp, zm, dpart, dall, dbuf, work,
    hsem, xs, xr, rsend, rrecv, ysend, yrecv, zsend, zrecv, esend, erecv, dsend, drecv, known,
):
    layer, c, x = lax.axis_index("layer"), lax.axis_index("row"), lax.axis_index("col")
    y, z = layer // NZ, layer % NZ
    right, left = (x + 1) % NX, (x + NX - 1) % NX
    up, down = (y + 1) % NY * NZ + z, (y + NY - 1) % NY * NZ + z
    ahead, behind = y * NZ + (z + 1) % NZ, y * NZ + (z + NZ - 1) % NZ

    def strip_of(order):
        return (y + 2 - order - order // 2 + 2 * (order // 3) + NY) % NY

    def place_of(t):
        late = t // 9
        return (1 - late) * (t % 3) + 3 * late, (1 - late) * (t // 3) + late * (t - 9)

    def remote(src, dst, send, recv, device):
        return pltpu.make_async_remote_copy(
            src_ref=src, dst_ref=dst, send_sem=send, recv_sem=recv, device_id=device, device_id_type=MESH
        )

    def load_left(order):
        strip = strip_of(order)
        return pltpu.make_async_copy(
            l_hbm.at[:, :, pl.ds(pl.multiple_of(strip * STRIP, BLK), STRIP)], lin.at[order], hsem.at[order]
        )

    load_right = pltpu.make_async_copy(r_hbm, rin, hsem.at[4])
    load_anc = pltpu.make_async_copy(anc_hbm.at[pl.ds(pl.multiple_of(layer * 48, 8), 48), :], anc, hsem.at[5])

    def xcopy(kind, t):
        order, s = place_of(t)
        b = strip_of(order)
        if kind == 0:
            src, dst, to = lbuf.at[0, b, s], lbuf.at[1, b, s], right
        elif kind == 1:
            src, dst, to = lbuf.at[0, b, s], lbuf.at[2, b, s], left
        elif kind == 2:
            src, dst, to = lbuf.at[1, b, s, 0:4], lbuf.at[3, b, s, 0:4], right
        else:
            src, dst, to = lbuf.at[2, b, s, 4:8], lbuf.at[3, b, s, 4:8], left
        return remote(src, dst, xs.at[kind, t], xr.at[kind, t], {"col": to})

    def rcopy(h, core):
        return remote(rbuf.at[2 * core + h], rbuf.at[2 * core + h], rsend.at[h], rrecv.at[h], {"row": 1 - c})

    def ycopy(kind, s):
        if kind == 0:
            src, dst, to = pbuf.at[3 * s, :, 0:HALF], ya.at[s], up
        elif kind == 1:
            src, dst, to = pbuf.at[3 * s, :, HALF:COLS], yb.at[s], down
        elif kind == 2:
            src, dst, to = pbuf.at[3 * s + 1], yp.at[s], up
        else:
            src, dst, to = pbuf.at[3 * s + 2], ym.at[s], down
        return remote(src, dst, ysend.at[kind, s], yrecv.at[kind, s], {"layer": to})

    def zcopy(way, s, h):
        if way == 0:
            block, to, landing = (z + 4 - h) % NZ, ahead, zp
            cut = pl.ds(HALF, HALF)
        else:
            block, to, landing = (z + 4 + h) % NZ, behind, zm
            cut = pl.ds(0, HALF)
        if h == 0:
            src, dst = zbuf.at[s, block, :, cut], landing.at[4 * s, :, cut]
        else:
            src, dst = zbuf.at[s, block], landing.at[4 * s + h]
        return remote(src, dst, zsend.at[way, 4 * s + h], zrecv.at[way, 4 * s + h], {"layer": to})

    yy = y % 2

    def ecopy(s, i, source, target):
        return remote(dpart.at[s], dall.at[s, source], esend.at[s, i], erecv.at[s, i], {"layer": y * NZ + target})

    def dcopy(s, half, i):
        to = (c * NY + y + i) % (2 * NY)
        return remote(
            dbuf.at[half, :, s], dbuf.at[half, :, s], dsend.at[s, i], drecv.at[half, s],
            {"layer": to % NY * NZ + z, "row": to // NY},
        )

    def load_blocks(j):
        return pltpu.make_async_copy(
            anc_hbm.at[pl.ds(pl.multiple_of(y * STRIP + j * BLK, BLK), BLK), pl.ds(pl.multiple_of((3 * yy + j) * BLK, BLK), BLK)],
            ancd.at[pl.ds(j * BLK, BLK), :],
            hsem.at[6 + j],
        )

    load_left(0).start()
    barrier = pltpu.get_barrier_semaphore()
    for to in ({"col": left}, {"col": right}, {"row": 1 - c}, {"layer": up}, {"layer": down}, {"layer": ahead}, {"layer": behind}):
        pl.semaphore_signal(barrier, inc=1, device_id=to, device_id_type=MESH)
    load_right.start()
    for order in range(1, NY):
        load_left(order).start()
    load_anc.start()
    for j in range(3):
        load_blocks(j).start()

    def tell(i):
        for to in (ahead, behind):
            pl.semaphore_signal(known.at[i], inc=1, device_id={"layer": to}, device_id_type=MESH)

    def prepare_left(order):
        b = strip_of(order)
        load_left(order).wait()
        for j in range(STRIP // BLK):
            pieces = []
            for k in range(SUPER):
                tile = lin[order, k, :, j * BLK : (j + 1) * BLK]
                pieces.append(jnp.where(lpat[k, 3 * b + j] > 0, tile, jnp.zeros_like(tile)))
            turned = jnp.concatenate(pieces, axis=0).T
            for g in range(8):
                place = 8 * j + g
                lbuf[0, b, place % PARTS, place // PARTS] = turned[g * GROUP : (g + 1) * GROUP, :]

    prepare_left(0)
    pl.semaphore_wait(barrier, 7)
    tell(0)
    xcopy(0, 0).start()
    xcopy(1, 0).start()
    load_right.wait()
    for k in range(SUPER):
        for j in range(COLS // BLK):
            for h in range(2):
                tile = rin[k, h * PIECE : (h + 1) * PIECE, j * BLK : (j + 1) * BLK]
                rbuf[2 * c + h, k * PIECE : (k + 1) * PIECE, j * BLK : (j + 1) * BLK] = jnp.where(
                    upat[j, 0, k] > 0, tile, jnp.zeros_like(tile)
                )
    for h in range(2):
        rcopy(h, c).start()
    for order in range(1, NY):
        prepare_left(order)
        if order < LEAD:
            xcopy(0, order).start()
            xcopy(1, order).start()

    owner = jnp.logical_and(c == x // 2, y // 2 == x % 2)

    def sum_y(s):
        ycopy(2, s).wait_recv()
        ycopy(3, s).wait_recv()
        zbuf[s] = (pbuf[9 + s] + yp[s] + ym[s]).reshape(NZ, GROUP, COLS)

        @pl.when(owner)
        def _():
            for block in range(NZ):
                j = 3 * yy + (48 * block + GROUP * s) // BLK
                piece = zbuf[s, block, :, pl.ds(pl.multiple_of(j * BLK, BLK), BLK)]
                dpart[s, block] = piece
                dall[s, z, block] = piece
            for i in range(1, NZ):
                ecopy(s, i, z, (z + i) % NZ).start()

    def share(s):
        @pl.when(owner)
        def _():
            for i in range(1, NZ):
                ecopy(s, i, (z + NZ - i) % NZ, z).wait_recv()
            for block in range(NZ):
                total = dall[s, 0, block]
                for source in range(1, NZ):
                    total = total + dall[s, source, block]
                rows = pl.ds(pl.multiple_of(48 * block + GROUP * s, GROUP), GROUP)
                dbuf[yy, block, s] = ancd[rows, :] - total
            for i in range(1, 2 * NY):
                dcopy(s, yy, i).start()

    def z_step(s, h):
        for way in range(2):
            block = (z + 4 - h) % NZ if way == 0 else (z + 4 + h) % NZ
            landing = zp if way == 0 else zm
            cut = slice(HALF, COLS) if way == 0 else slice(0, HALF)
            if h >= 1:
                zcopy(way, s, h - 1).wait_recv()
            if h == 1:
                zbuf[s, block, :, cut] = zbuf[s, block, :, cut] + landing[4 * s, :, cut]
            elif 1 < h < 4:
                zbuf[s, block] = zbuf[s, block] + landing[4 * s + h - 1]
            if h < 4:
                zcopy(way, s, h).start()
        if h == 4:
            rows = pl.ds(GROUP * s if isinstance(s, int) else pl.multiple_of(GROUP * s, GROUP), GROUP)
            schur_ref[rows, :] = anc[rows, :] - (zbuf[s, z] + zp[4 * s + 3] + zm[4 * s + 3])

    def step(t, carry):
        @pl.when(t < CHUNKS)
        def _():
            xcopy(0, t).wait_recv()
            xcopy(2, t).start()
            xcopy(1, t).wait_recv()
            xcopy(3, t).start()

        @pl.when(t < CHUNKS - LEAD)
        def _():
            xcopy(0, t + LEAD).start()
            xcopy(1, t + LEAD).start()

        for i in range(3):

            @pl.when(t == i + 2)
            def _():
                pl.semaphore_wait(known.at[i], 2)
                if i < 2:
                    tell(i + 1)

        @pl.when(t == 1)
        def _():
            for h in range(2):
                rcopy(h, 1 - c).wait_recv()
            load_anc.wait()
            for j in range(3):
                load_blocks(j).wait()

        @pl.when(jnp.logical_and(t >= 1, t < CHUNKS + 1))
        def _():
            u = t - 1
            xcopy(2, u).wait_recv()
            xcopy(3, u).wait_recv()
            order, s = place_of(u)
            b = strip_of(order)
            for n in range(COLS // 256):
                total = None
                for slot, shift in enumerate((0, 3, 1, 2)):
                    product = jnp.dot(
                        lbuf[slot, b, s].reshape(HEIGHT, SUPER * PIECE),
                        rbuf[(x + shift) % NX, :, n * 256 : (n + 1) * 256],
                        preferred_element_type=jnp.float32,
                    )
                    total = product if total is None else total + product
                pbuf[u, :, n * 256 : (n + 1) * 256] = total

            @pl.when(order == 0)
            def _():
                ycopy(0, s).start()
                ycopy(1, s).start()

            @pl.when(order == 2)
            def _():
                ycopy(1, s).wait_recv()
                pbuf[u, :, HALF:COLS] = pbuf[u, :, HALF:COLS] + yb[s]
                ycopy(3, s).start()

        @pl.when(jnp.logical_and(t >= 2, jnp.logical_and(t < 11, (t - 2) % 3 == 1)))
        def _():
            v = t - 2
            ycopy(0, v // 3).wait_recv()
            pbuf[v, :, 0:HALF] = pbuf[v, :, 0:HALF] + ya[v // 3]
            ycopy(2, v // 3).start()

        for h in range(2, 5):
            late = t - START - h

            @pl.when(jnp.logical_and(late >= 0, late < PARTS))
            def _():
                z_step(late, h)

        for h in range(2):
            early = t - START - h

            @pl.when(jnp.logical_and(early >= 0, early < PARTS))
            def _():
                if h == 0:
                    sum_y(early)
                z_step(early, h)
                if h == 1:
                    share(early)

        return carry

    lax.fori_loop(0, START + PARTS + 1, step, 0)
    z_step(0, 4)
    z_step(1, 3)
    z_step(2, 2)
    for half in range(2):

        @pl.when(jnp.logical_not(jnp.logical_and(owner, yy == half)))
        def _():
            for s in range(PARTS):
                dcopy(s, half, 1).wait_recv()

    work[...] = dbuf[...].reshape(6, BLK, BLK)
    lu_segment(0, work, part_ref)
    z_step(1, 4)
    z_step(2, 3)
    lu_segment(1, work, part_ref)
    z_step(2, 4)
    lu_segment(2, work, part_ref)
    rest_ref[...] = work[:, 0 : BLK // SEGMENTS, :]

    @pl.when(owner)
    def _():
        for s in range(PARTS):
            for i in range(1, NZ):
                ecopy(s, i, z, (z + i) % NZ).wait_send()
            for i in range(1, 2 * NY):
                dcopy(s, yy, i).wait_send()

    for h in range(2):
        rcopy(h, c).wait_send()

    def drain_x(t, carry):
        for kind in range(4):
            xcopy(kind, t).wait_send()
        return carry

    lax.fori_loop(0, CHUNKS, drain_x, 0)

    def drain_yz(s, carry):
        for kind in range(4):
            ycopy(kind, s).wait_send()
        for h in range(4):
            for way in range(2):
                zcopy(way, s, h).wait_send()
        return carry

    lax.fori_loop(0, PARTS, drain_yz, 0)


def shards(lpanel, upanel, lpat, upat, ancestor_entries):
    f32, bf16 = jnp.float32, jnp.bfloat16
    vmem = pl.BlockSpec(memory_space=pltpu.VMEM)
    smem = pl.BlockSpec(memory_space=pltpu.SMEM)
    anywhere = pl.BlockSpec(memory_space=pl.ANY)
    dma = pltpu.SemaphoreType.DMA
    exchange = pl.pallas_call(
        kernel,
        out_shape=(
            jax.ShapeDtypeStruct((48, COLS), f32),
            jax.ShapeDtypeStruct((6, BLK, BLK), f32),
            jax.ShapeDtypeStruct((6, BLK // SEGMENTS, BLK), f32),
        ),
        in_specs=[anywhere, anywhere, smem, smem, anywhere],
        out_specs=(vmem, vmem, vmem),
        scratch_shapes=[
            pltpu.VMEM((NY, SUPER, PIECE, STRIP), bf16),
            pltpu.VMEM((SUPER, 2 * PIECE, COLS), bf16),
            pltpu.VMEM((48, COLS), f32),
            pltpu.VMEM((STRIP, BLK), f32),
            pltpu.VMEM((NX, NY, PARTS, NZ, GROUP, SUPER * PIECE), bf16),
            pltpu.VMEM((NX, SUPER * PIECE, COLS), bf16),
            pltpu.VMEM((CHUNKS, HEIGHT, COLS), f32),
            pltpu.VMEM((PARTS, HEIGHT, HALF), f32),
            pltpu.VMEM((PARTS, HEIGHT, HALF), f32),
            pltpu.VMEM((PARTS, HEIGHT, COLS), f32),
            pltpu.VMEM((PARTS, HEIGHT, COLS), f32),
            pltpu.VMEM((PARTS, NZ, GROUP, COLS), f32),
            pltpu.VMEM((4 * PARTS, GROUP, COLS), f32),
            pltpu.VMEM((4 * PARTS, GROUP, COLS), f32),
            pltpu.VMEM((PARTS, NZ, GROUP, BLK), f32),
            pltpu.VMEM((PARTS, NZ, NZ, GROUP, BLK), f32),
            pltpu.VMEM((2, NZ, PARTS, GROUP, BLK), f32),
            pltpu.VMEM((6, BLK, BLK), f32),
            dma((9,)), dma((4, CHUNKS)), dma((4, CHUNKS)), dma((2,)), dma((2,)),
            dma((4, PARTS)), dma((4, PARTS)), dma((2, 4 * PARTS)), dma((2, 4 * PARTS)),
            dma((PARTS, NZ)), dma((PARTS, NZ)), dma((PARTS, 2 * NY)), dma((2, PARTS)), pltpu.SemaphoreType.REGULAR((3,)),
        ],
        compiler_params=pltpu.CompilerParams(
            collective_id=0, has_side_effects=True, vmem_limit_bytes=60 * 1024 * 1024
        ),
    )
    schur, part, rest = exchange(
        jnp.swapaxes(lpanel[0], 1, 2),
        upanel[0],
        lpat[0],
        jnp.transpose(upat, (2, 0, 1)),
        ancestor_entries,
    )
    return pl.pallas_call(
        finish_kernel,
        out_shape=(jax.ShapeDtypeStruct(schur.shape, f32), jax.ShapeDtypeStruct(part.shape, f32)),
        in_specs=[vmem, vmem, vmem],
        out_specs=(vmem, vmem),
        scratch_shapes=[pltpu.VMEM(rest.shape, f32)],
    )(schur, part, rest)


def solution(mesh):
    return jax.shard_map(
        shards,
        mesh=mesh,
        in_specs=(
            P("layer", None, "row", "col"),
            P("layer", None, "row", "col"),
            P("layer", None, "row"),
            P("layer", None, "col"),
            P("row", "col"),
        ),
        out_specs=(P(("row", "layer"), "col"), P("col", None, None)),
        check_vma=False,
    )
```

time: 152 us -> 115 us (0.76); the launches traced: 151 us -> 115 us
  Pallas kernels: 145 us -> 115 us
  local copies, waits for them, and re-layouts: 4.62 us -> 0 us
    pallas_call x1 -> x2, Pallas kernels: 145 us -> 115 us  [the longest x1 109 us: shards(): exchange(jnp.swapaxes(lpanel[0], 1, 2), upanel[0], lpat[0], jnp.transpose...]
    unnamed x2 -> x0, local copies, waits for them, and re-layouts: 3.35 us -> none
where the time goes in v3:
time: 115 us
  Pallas kernels  115 us (100%)
    pallas_call x1, Pallas kernels, shards(): exchange(jnp.swapaxes(lpanel[0], 1, 2), upanel[0], lpat[0], jnp.transpose...  109 us
    pallas_call x1, Pallas kernels, shards(): pl.pallas_call(finish_kernel, out_shape=(jax.ShapeDtypeStruct(schur.shape...  5.16 us

profile of v3, /device:TPU:2, one launch (start us, length us, event | category | flops | bytes accessed | tf_op | source)
XLA Modules:
  0.0 115.2 jit_solution(13794305347785264890)
XLA Ops:
  0.6 109.4 %shard_map.68 = (f32[48,768]{1,0:T(8,128)}, f32[6,128,128]{2,1,0:T(8,128)}, f32[6,32,128]{2,1,0:T(8,128)}) custom-call(bf16[8,64,1536]{2,1,0:T(8,128)(2,1)} %bitcast.6, bf16[8,128,768]{2,1,0:T(8,128)(2,1)} %bitcast.7, s32[8,12]{1,0:T(8,128)} %bitcast.8, s32[6,1,8]{2,1,0:T(1,128)} %bitcast.9, f32[1536,768]{1,0:T(8,128)} %anc_hbm.1), custom_call_target="tpu_custom_call" | custom-call | tf_op jit(solution)/shard_map/pallas_call | solution.py:437
  110.1 5.2 %shard_map.69 = (f32[48,768]{1,0:T(8,128)}, f32[6,128,128]{2,1,0:T(8,128)}) custom-call(f32[48,768]{1,0:T(8,128)} %get-tuple-element.5.schur_ref, f32[6,128,128]{2,1,0:T(8,128)} %get-tuple-element.6.part_ref, f32[6,32,128]{2,1,0:T(8,128)} %get-tuple-element.7.rest_ref), custom_call_target="tpu_custom_call" | custom-call | tf_op jit(solution)/shard_map/pallas_call | solution.py:444

commit v4 on v3

--- a/solution.py
+++ b/solution.py
@@ -73,7 +73,7 @@
 def kernel(
     l_hbm, r_hbm, lpat, upat, anc_hbm, schur_ref, part_ref, rest_ref,
     lin, rin, anc, ancd, lbuf, rbuf, pbuf, ya, yb, yp, ym, zbuf, zp, zm, dpart, dall, dbuf, work,
-    hsem, xs, xr, rsend, rrecv, ysend, yrecv, zsend, zrecv, esend, erecv, dsend, drecv, known,
+    hsem, xs, xr, rsend, rrecv, ysend, yrecv, zsend, zrecv, esend, erecv, fsend, frecv, dsend, drecv, known,
 ):
     layer, c, x = lax.axis_index("layer"), lax.axis_index("row"), lax.axis_index("col")
     y, z = layer // NZ, layer % NZ
@@ -145,7 +145,14 @@
     yy = y % 2
 
     def ecopy(s, i, source, target):
-        return remote(dpart.at[s], dall.at[s, source], esend.at[s, i], erecv.at[s, i], {"layer": y * NZ + target})
+        return remote(
+            dpart.at[s, target], dall.at[s, source], esend.at[s, i], erecv.at[s, i], {"layer": y * NZ + target}
+        )
+
+    def fcopy(s, i, source, target):
+        return remote(
+            dbuf.at[yy, source, s], dbuf.at[yy, source, s], fsend.at[s, i], frecv.at[s, i], {"layer": y * NZ + target}
+        )
 
     def dcopy(s, half, i):
         to = (c * NY + y + i) % (2 * NY)
@@ -221,9 +228,8 @@
         def _():
             for block in range(NZ):
                 j = 3 * yy + (48 * block + GROUP * s) // BLK
-                piece = zbuf[s, block, :, pl.ds(pl.multiple_of(j * BLK, BLK), BLK)]
-                dpart[s, block] = piece
-                dall[s, z, block] = piece
+                dpart[s, block] = zbuf[s, block, :, pl.ds(pl.multiple_of(j * BLK, BLK), BLK)]
+            dall[s, z] = dpart[s, z]
             for i in range(1, NZ):
                 ecopy(s, i, z, (z + i) % NZ).start()
 
@@ -232,12 +238,19 @@
         def _():
             for i in range(1, NZ):
                 ecopy(s, i, (z + NZ - i) % NZ, z).wait_recv()
-            for block in range(NZ):
-                total = dall[s, 0, block]
-                for source in range(1, NZ):
-                    total = total + dall[s, source, block]
-                rows = pl.ds(pl.multiple_of(48 * block + GROUP * s, GROUP), GROUP)
-                dbuf[yy, block, s] = ancd[rows, :] - total
+            total = dall[s, 0]
+            for source in range(1, NZ):
+                total = total + dall[s, source]
+            rows = pl.ds(pl.multiple_of(48 * z + GROUP * s, GROUP), GROUP)
+            dbuf[yy, z, s] = ancd[rows, :] - total
+            for i in range(1, NZ):
+                fcopy(s, i, z, (z + i) % NZ).start()
+
+    def hand_out(s):
+        @pl.when(owner)
+        def _():
+            for i in range(1, NZ):
+                fcopy(s, i, (z + NZ - i) % NZ, z).wait_recv()
             for i in range(1, 2 * NY):
                 dcopy(s, yy, i).start()
 
@@ -323,7 +336,7 @@
             pbuf[v, :, 0:HALF] = pbuf[v, :, 0:HALF] + ya[v // 3]
             ycopy(2, v // 3).start()
 
-        for h in range(2, 5):
+        for h in range(2, 4):
             late = t - START - h
 
             @pl.when(jnp.logical_and(late >= 0, late < PARTS))
@@ -341,12 +354,21 @@
                 if h == 1:
                     share(early)
 
+        @pl.when(jnp.logical_and(t >= START + 2, t < START + PARTS))
+        def _():
+            hand_out(t - START - 2)
+
         return carry
 
-    lax.fori_loop(0, START + PARTS + 1, step, 0)
+    lax.fori_loop(0, START + PARTS, step, 0)
+    share(2)
+    z_step(2, 1)
+    hand_out(1)
+    hand_out(2)
+    z_step(0, 3)
+    z_step(1, 2)
+    z_step(2, 2)
     z_step(0, 4)
-    z_step(1, 3)
-    z_step(2, 2)
     for half in range(2):
 
         @pl.when(jnp.logical_not(jnp.logical_and(owner, yy == half)))
@@ -356,9 +378,10 @@
 
     work[...] = dbuf[...].reshape(6, BLK, BLK)
     lu_segment(0, work, part_ref)
-    z_step(1, 4)
+    z_step(1, 3)
     z_step(2, 3)
     lu_segment(1, work, part_ref)
+    z_step(1, 4)
     z_step(2, 4)
     lu_segment(2, work, part_ref)
     rest_ref[...] = work[:, 0 : BLK // SEGMENTS, :]
@@ -368,6 +391,7 @@
         for s in range(PARTS):
             for i in range(1, NZ):
                 ecopy(s, i, z, (z + i) % NZ).wait_send()
+                fcopy(s, i, z, (z + i) % NZ).wait_send()
             for i in range(1, 2 * NY):
                 dcopy(s, yy, i).wait_send()
 
@@ -423,12 +447,12 @@
             pltpu.VMEM((4 * PARTS, GROUP, COLS), f32),
             pltpu.VMEM((4 * PARTS, GROUP, COLS), f32),
             pltpu.VMEM((PARTS, NZ, GROUP, BLK), f32),
-            pltpu.VMEM((PARTS, NZ, NZ, GROUP, BLK), f32),
+            pltpu.VMEM((PARTS, NZ, GROUP, BLK), f32),
             pltpu.VMEM((2, NZ, PARTS, GROUP, BLK), f32),
             pltpu.VMEM((6, BLK, BLK), f32),
             dma((9,)), dma((4, CHUNKS)), dma((4, CHUNKS)), dma((2,)), dma((2,)),
             dma((4, PARTS)), dma((4, PARTS)), dma((2, 4 * PARTS)), dma((2, 4 * PARTS)),
-            dma((PARTS, NZ)), dma((PARTS, NZ)), dma((PARTS, 2 * NY)), dma((2, PARTS)), pltpu.SemaphoreType.REGULAR((3,)),
+            dma((PARTS, NZ)), dma((PARTS, NZ)), dma((PARTS, NZ)), dma((PARTS, NZ)), dma((PARTS, 2 * NY)), dma((2, PARTS)), pltpu.SemaphoreType.REGULAR((3,)),
         ],
         compiler_params=pltpu.CompilerParams(
             collective_id=0, has_side_effects=True, vmem_limit_bytes=60 * 1024 * 1024

time: 115 us -> 107 us (0.930)
  Pallas kernels: 115 us -> 106 us
    pallas_call x1, Pallas kernels: 109 us -> 101 us  [shards(): exchange(jnp.swapaxes(lpanel[0], 1, 2), upanel[0], lpat[0], jnp.transpose...]
where the time goes in v4:
time: 107 us; the launch traced here: 106 us
  Pallas kernels  106 us (99%)
    pallas_call x1, Pallas kernels, shards(): exchange(jnp.swapaxes(lpanel[0], 1, 2), upanel[0], lpat[0], jnp.transpose...  101 us
    pallas_call x1, Pallas kernels, shards(): pl.pallas_call(finish_kernel, out_shape=(jax.ShapeDtypeStruct(schur.shape...  5.16 us

profile of v4, /device:TPU:2, one launch (start us, length us, event | category | flops | bytes accessed | tf_op | source)
XLA Modules:
  0.0 106.4 jit_solution(11652134571805319158)
XLA Ops:
  0.6 100.6 %shard_map.68 = (f32[48,768]{1,0:T(8,128)}, f32[6,128,128]{2,1,0:T(8,128)}, f32[6,32,128]{2,1,0:T(8,128)}) custom-call(bf16[8,64,1536]{2,1,0:T(8,128)(2,1)} %bitcast.6, bf16[8,128,768]{2,1,0:T(8,128)(2,1)} %bitcast.7, s32[8,12]{1,0:T(8,128)} %bitcast.8, s32[6,1,8]{2,1,0:T(1,128)} %bitcast.9, f32[1536,768]{1,0:T(8,128)} %anc_hbm.1), custom_call_target="tpu_custom_call" | custom-call | tf_op jit(solution)/shard_map/pallas_call | solution.py:461
  101.2 5.2 %shard_map.69 = (f32[48,768]{1,0:T(8,128)}, f32[6,128,128]{2,1,0:T(8,128)}) custom-call(f32[48,768]{1,0:T(8,128)} %get-tuple-element.5.schur_ref, f32[6,128,128]{2,1,0:T(8,128)} %get-tuple-element.6.part_ref, f32[6,32,128]{2,1,0:T(8,128)} %get-tuple-element.7.rest_ref), custom_call_target="tpu_custom_call" | custom-call | tf_op jit(solution)/shard_map/pallas_call | solution.py:468

commit v5 on v4

--- a/solution.py
+++ b/solution.py
@@ -19,7 +19,7 @@
 CHUNKS = NY * PARTS
 HEIGHT = NZ * GROUP
 STRIP = NZ * GROUP * PARTS
-LEAD = 3
+LEAD = 2
 START = 10
 
 
@@ -151,13 +151,13 @@
 
     def fcopy(s, i, source, target):
         return remote(
-            dbuf.at[yy, source, s], dbuf.at[yy, source, s], fsend.at[s, i], frecv.at[s, i], {"layer": y * NZ + target}
+            dbuf.at[:, source, s], dbuf.at[:, source, s], fsend.at[s, i], frecv.at[s, i], {"layer": y * NZ + target}
         )
 
     def dcopy(s, half, i):
         to = (c * NY + y + i) % (2 * NY)
         return remote(
-            dbuf.at[half, :, s], dbuf.at[half, :, s], dsend.at[s, i], drecv.at[half, s],
+            dbuf.at[half, z, s], dbuf.at[half, z, s], dsend.at[s, i], drecv.at[half, s],
             {"layer": to % NY * NZ + z, "row": to // NY},
         )
 
@@ -243,16 +243,18 @@
                 total = total + dall[s, source]
             rows = pl.ds(pl.multiple_of(48 * z + GROUP * s, GROUP), GROUP)
             dbuf[yy, z, s] = ancd[rows, :] - total
-            for i in range(1, NZ):
-                fcopy(s, i, z, (z + i) % NZ).start()
-
-    def hand_out(s):
-        @pl.when(owner)
-        def _():
-            for i in range(1, NZ):
-                fcopy(s, i, (z + NZ - i) % NZ, z).wait_recv()
             for i in range(1, 2 * NY):
                 dcopy(s, yy, i).start()
+
+    def hand_out(s):
+        for half in range(2):
+
+            @pl.when(jnp.logical_not(jnp.logical_and(owner, yy == half)))
+            def _():
+                dcopy(s, half, 1).wait_recv()
+
+        for i in range(1, NZ):
+            fcopy(s, i, z, (z + i) % NZ).start()
 
     def z_step(s, h):
         for way in range(2):
@@ -369,12 +371,9 @@
     z_step(1, 2)
     z_step(2, 2)
     z_step(0, 4)
-    for half in range(2):
-
-        @pl.when(jnp.logical_not(jnp.logical_and(owner, yy == half)))
-        def _():
-            for s in range(PARTS):
-                dcopy(s, half, 1).wait_recv()
+    for s in range(PARTS):
+        for i in range(1, NZ):
+            fcopy(s, i, (z + NZ - i) % NZ, z).wait_recv()
 
     work[...] = dbuf[...].reshape(6, BLK, BLK)
     lu_segment(0, work, part_ref)
@@ -391,10 +390,12 @@
         for s in range(PARTS):
             for i in range(1, NZ):
                 ecopy(s, i, z, (z + i) % NZ).wait_send()
-                fcopy(s, i, z, (z + i) % NZ).wait_send()
             for i in range(1, 2 * NY):
                 dcopy(s, yy, i).wait_send()
 
+    for s in range(PARTS):
+        for i in range(1, NZ):
+            fcopy(s, i, z, (z + i) % NZ).wait_send()
     for h in range(2):
         rcopy(h, c).wait_send()
 

time: 107 us -> 104 us (0.972)
  Pallas kernels: 106 us -> 104 us
    pallas_call x1, Pallas kernels: 101 us -> 98.5 us  [shards(): exchange(jnp.swapaxes(lpanel[0], 1, 2), upanel[0], lpat[0], jnp.transpose...]
where the time goes in v5:
time: 104 us
  Pallas kernels  104 us (100%)
    pallas_call x1, Pallas kernels, shards(): exchange(jnp.swapaxes(lpanel[0], 1, 2), upanel[0], lpat[0], jnp.transpose...  98.5 us
    pallas_call x1, Pallas kernels, shards(): pl.pallas_call(finish_kernel, out_shape=(jax.ShapeDtypeStruct(schur.shape...  5.16 us

profile of v5, /device:TPU:2, one launch (start us, length us, event | category | flops | bytes accessed | tf_op | source)
XLA Modules:
  0.0 104.3 jit_solution(437175184236975164)
XLA Ops:
  0.6 98.5 %shard_map.68 = (f32[48,768]{1,0:T(8,128)}, f32[6,128,128]{2,1,0:T(8,128)}, f32[6,32,128]{2,1,0:T(8,128)}) custom-call(bf16[8,64,1536]{2,1,0:T(8,128)(2,1)} %bitcast.6, bf16[8,128,768]{2,1,0:T(8,128)(2,1)} %bitcast.7, s32[8,12]{1,0:T(8,128)} %bitcast.8, s32[6,1,8]{2,1,0:T(1,128)} %bitcast.9, f32[1536,768]{1,0:T(8,128)} %anc_hbm.1), custom_call_target="tpu_custom_call" | custom-call | tf_op jit(solution)/shard_map/pallas_call | solution.py:462
  99.1 5.2 %shard_map.69 = (f32[48,768]{1,0:T(8,128)}, f32[6,128,128]{2,1,0:T(8,128)}) custom-call(f32[48,768]{1,0:T(8,128)} %get-tuple-element.5.schur_ref, f32[6,128,128]{2,1,0:T(8,128)} %get-tuple-element.6.part_ref, f32[6,32,128]{2,1,0:T(8,128)} %get-tuple-element.7.rest_ref), custom_call_target="tpu_custom_call" | custom-call | tf_op jit(solution)/shard_map/pallas_call | solution.py:469
